TPU v7x, 32 devices: a whole 2x2x4 slice. The times are simulated.
32 devices in a mesh: league: 4 (over x, core), env: 8 (over z, y).
Axes of the slice: x: 2, y: 2, z: 4, core: 2. Of those that a mesh axis runs over, the one named last changes fastest.
Arguments:
- obs_own: bfloat16 [4, 2, 128, 16, 2048], P('league', None, 'env'), may hold values from -6 to 6
- obs_opp: bfloat16 [4, 2, 128, 16, 2048], P('league', None, 'env'), may hold values from -6 to 6
- actions: int32 [4, 2, 2, 128, 16], P('league', None, None, 'env'), may hold values from 0 to 255
- opponent_picks: int32 [4, 2], P('league'), may hold values from 0 to 3
- policy_weight: bfloat16 [4, 2048, 2048], P('league', 'env'), may hold values from -0.125 to 0.125
- policy_gain: bfloat16 [4, 2048], P('league'), may hold values from 0.25 to 1.75
- action_table: bfloat16 [256, 2048], replicated, may hold values from -6 to 6
- value_gain: bfloat16 [2048], replicated, may hold values from 0.25 to 1.75
- value_up: bfloat16 [2048, 1024], replicated, may hold values from -0.125 to 0.125
- value_out: bfloat16 [1024], replicated, may hold values from -0.1875 to 0.1875
Outputs:
- learner_rows: bfloat16 [4, 2, 16, 2048, 128], P('league', None, None, 'env')
- values: float32 [4, 2, 128, 16], P('league', None, 'env')
All inputs are finite; a program needn't handle non-finite values.
Results may differ from a plain program's by a relative error of at most 0.0054.
Values may be sent and summed in bfloat16 or wider, within the bound.
A program may use at most 128 MiB of HBM per device.

v0:
```python
import jax
import jax.numpy as jnp
from jax import lax
from jax.sharding import PartitionSpec as P


def rms_norm(inputs, gain):
    scale = lax.rsqrt(jnp.mean(inputs * inputs, axis=-1, keepdims=True) + 1e-05)
    return inputs * scale * gain.astype(jnp.float32)


def local(
    obs_own,
    obs_opp,
    actions,
    opponent_picks,
    policy_weight,
    policy_gain,
    action_table,
    value_gain,
    value_up,
    value_out,
):
    round_count = obs_own.shape[1]
    env_count = obs_own.shape[2]
    step_count = obs_own.shape[3]
    model_width = obs_own.shape[4]
    row_count = env_count * step_count
    weight_shard = policy_weight[0]
    own_gain = policy_gain[0]
    group_count = lax.axis_size("league")
    my_group = lax.axis_index("league")
    own_inputs = obs_own[0].reshape(round_count * row_count, model_width).astype(jnp.float32)
    own_normed = rms_norm(own_inputs, own_gain).astype(jnp.bfloat16)
    own_whole = lax.all_gather(weight_shard, "env", axis=0, tiled=True)
    own_state = own_inputs + jnp.dot(own_normed, own_whole, preferred_element_type=jnp.float32)
    every_pick = lax.all_gather(opponent_picks, "league", axis=0, tiled=True)
    action_range = jnp.arange(action_table.shape[0], dtype=jnp.int32)
    traj_list = []
    value_list = []
    for round_index in range(round_count):
        opp_raw = obs_opp[0, round_index].reshape(row_count, model_width)
        opp_inputs = opp_raw.astype(jnp.float32)
        all_rows = lax.all_gather(opp_raw, "league", axis=0, tiled=True)
        all_normed = rms_norm(all_rows.astype(jnp.float32), own_gain).astype(jnp.bfloat16)
        products = jnp.dot(all_normed, own_whole, preferred_element_type=jnp.float32)
        served = (every_pick[:, round_index] == my_group).astype(jnp.float32)
        products = (
            products.reshape(group_count, row_count, model_width) * served[:, None, None]
        ).astype(jnp.bfloat16)
        answers = lax.all_to_all(products, "league", split_axis=0, concat_axis=0, tiled=True)
        opp_state = opp_inputs + jnp.sum(answers.astype(jnp.float32), axis=0)
        own_ids = actions[0, 0, round_index].reshape(row_count)
        opp_ids = actions[0, 1, round_index].reshape(row_count)
        onehot = (own_ids[:, None] == action_range[None, :]).astype(jnp.bfloat16) + (
            opp_ids[:, None] == action_range[None, :]
        ).astype(jnp.bfloat16)
        action_sum = jnp.dot(onehot, action_table, preferred_element_type=jnp.float32)
        round_state = lax.dynamic_slice_in_dim(own_state, round_index * row_count, row_count, 0)
        joint_sum = round_state + opp_state + action_sum
        joint_row = rms_norm(joint_sum, value_gain).astype(jnp.bfloat16)
        value_hidden = jax.nn.silu(
            jnp.dot(joint_row, value_up, preferred_element_type=jnp.float32)
        ).astype(jnp.bfloat16)
        value_est = jnp.dot(value_hidden, value_out, preferred_element_type=jnp.float32)
        value_list.append(value_est.reshape(env_count, step_count))
        time_block = joint_row.reshape(env_count, step_count, model_width).transpose(1, 2, 0)
        traj_list.append(lax.all_to_all(time_block, "env", split_axis=1, concat_axis=2, tiled=True))
    learner_rows = jnp.stack(traj_list)
    values = jnp.stack(value_list)
    return (learner_rows[None], values[None])


def solution(mesh):
    in_specs = (
        P("league", None, "env", None, None),
        P("league", None, "env", None, None),
        P("league", None, None, "env", None),
        P("league", None),
        P("league", "env", None),
        P("league", None),
        P(),
        P(),
        P(),
        P(),
    )
    out_specs = (P("league", None, None, "env", None), P("league", None, "env", None))
    return jax.shard_map(local, mesh=mesh, in_specs=in_specs, out_specs=out_specs, check_vma=False)
```

profile of v0, /device:TPU:0, one launch (start us, length us, event | category | flops | bytes accessed | tf_op | source)
XLA Modules:
  0.0 430.5 jit_solution(11888221236370943280)
XLA Ops:
  7.2 3.2 fusion.43
  10.5 0.7 all-gather.10.cloned.1.call-update
  11.3 0.7 all-gather.8.cloned.1.call-update
  12.0 6.0 %all-gather.1 = s32[4,1,2]{2,1,0:T(1,128)S(1)} all-gather(s32[1,1,2]{2,1,0:T(1,128)S(1)} %bitcast.90), channel_id=1, replica_groups=mesh['league'=4,'env'=8] {'league'}, dimensions={0}, use_global_device_ids=true | all-gather | bytes 40 | tf_op jit(solution)/shard_map/all_gather | solution.py:37
  17.9 0.1 copy.23
  18.0 29.8 %all-gather.6.cloned.1.call-done = bf16[1024,2048]{1,0:T(8,128)(2,1)} async-done(((bf16[256,2048]{1,0:T(8,128)(2,1)}), bf16[1024,2048]{1,0:T(8,128)(2,1)}) %all-gather.6.cloned.1.call-update) | async-done | bytes 4194320 | tf_op jit(solution)/shard_map/all_gather | solution.py:44
  47.8 3.1 fusion
  50.9 124.0 %all-gather.10.cloned.1.call-done = bf16[1,2048,2048]{2,1,0:T(8,128)(2,1)} async-done(((bf16[1,256,2048]{2,1,0:T(8,128)(2,1)}), bf16[1,2048,2048]{2,1,0:T(8,128)(2,1)}) %all-gather.10.cloned.1.call-update) | async-done | bytes 8388624 | tf_op jit(solution)/shard_map/all_gather | solution.py:35
  174.9 12.6 %fusion.8 = f32[1024,2048]{1,0:T(8,128)S(1)} fusion(bf16[1,2048,2048]{2,1,0:T(8,128)(2,1)} %all-gather.10.cloned.1.call-done, bf16[1024,2048]{1,0:T(8,128)(2,1)} %all-gather.6.cloned.1.call-done, f32[2048]{0:T(1024)S(1)} %bitcast.84, f32[1024]{0:T(1024)S(1)} %add_rsqrt_fusion.2), kind=kOutput, calls=%fused_computation.12 | convolution fusion | flops 8598323200 | bytes 20983808 | tf_op jit(solution)/shard_map/dot_general | solution.py:46
  187.5 3.2 multiply_convert_fusion.1
  190.7 4.9 %all-to-all-start = ((bf16[4,256,2048]{2,1,0:T(8,128)(2,1)}), bf16[4,256,2048]{2,1,0:T(8,128)(2,1)}, u32[]{:S(2)}, u32[]{:S(2)}) async-start(bf16[4,256,2048]{2,1,0:T(8,128)(2,1)} %multiply_convert_fusion.1), calls=%async_computation | async-start | bytes 8388608 | tf_op jit(solution)/shard_map/all_to_all | solution.py:51
  195.6 22.4 %all-gather.8.cloned.1.call-done = bf16[1024,2048]{1,0:T(8,128)(2,1)} async-done(((bf16[256,2048]{1,0:T(8,128)(2,1)}), bf16[1024,2048]{1,0:T(8,128)(2,1)}) %all-gather.8.cloned.1.call-update) | async-done | bytes 4194320 | tf_op jit(solution)/shard_map/all_gather | solution.py:44
  218.0 3.2 fusion.3
  221.2 0.2 copy-done.7
  221.4 11.3 %fusion.6 = f32[1024,2048]{1,0:T(8,128)S(1)} fusion(bf16[1,2048,2048]{2,1,0:T(8,128)(2,1)} %all-gather.10.cloned.1.call-done, bf16[1024,2048]{1,0:T(8,128)(2,1)S(1)} %copy-done.7, f32[1024]{0:T(1024)S(1)} %add_rsqrt_fusion.1, f32[2048]{0:T(1024)S(1)} %bitcast.85), kind=kOutput, calls=%fused_computation.10 | convolution fusion | flops 8598323200 | bytes 20983808 | tf_op jit(solution)/shard_map/dot_general | solution.py:46
  232.7 3.2 multiply_convert_fusion
  235.9 16.6 %all-to-all-done = bf16[4,256,2048]{2,1,0:T(8,128)(2,1)} async-done(((bf16[4,256,2048]{2,1,0:T(8,128)(2,1)}), bf16[4,256,2048]{2,1,0:T(8,128)(2,1)}, u32[]{:S(2)}, u32[]{:S(2)}) %all-to-all-start) | async-done | bytes 4194336 | tf_op jit(solution)/shard_map/all_to_all | solution.py:51
  252.6 5.0 %all-to-all-start.2 = ((bf16[4,256,2048]{2,1,0:T(8,128)(2,1)}), bf16[4,256,2048]{2,1,0:T(8,128)(2,1)}, u32[]{:S(2)}, u32[]{:S(2)}) async-start(bf16[4,256,2048]{2,1,0:T(8,128)(2,1)} %multiply_convert_fusion), calls=%async_computation.2 | async-start | bytes 8388608 | tf_op jit(solution)/shard_map/all_to_all | solution.py:51
  257.6 0.1 eq.86
  257.8 0.5 fusion.14
  258.3 0.1 rsqrt.44
  258.4 0.1 eq.95
  258.6 0.5 fusion.16
  259.1 7.0 %bitcast_add_fusion = f32[512,2048]{1,0:T(8,128)S(1)} fusion(bf16[1,2,16,16,2048]{4,3,2,1,0:T(8,128)(2,1)S(1)} %copy-done.4, bf16[512,2048]{1,0:T(8,128)(2,1)S(1)} %fusion.16, bf16[1,2048,2048]{2,1,0:T(8,128)(2,1)} %all-gather.10.cloned.1.call-done), kind=kOutput, calls=%fused_computation.20 | convolution fusion | flops 4297064448 | bytes 16777216 | tf_op jit(solution)/shard_map/dot_general | solution.py:36
  266.1 4.8 %convert_reduce_fusion.1 = f32[256,2048]{1,0:T(8,128)S(1)} fusion(bf16[4,256,2048]{2,1,0:T(8,128)(2,1)} %all-to-all-done), kind=kLoop, calls=%fused_computation.18 | loop fusion | flops 3670016 | bytes 6291456 | tf_op jit(solution)/shard_map/reduce_sum | solution.py:52
  271.0 2.1 multiply_reduce_fusion.1
  273.1 32.6 %all-to-all-done.2 = bf16[4,256,2048]{2,1,0:T(8,128)(2,1)} async-done(((bf16[4,256,2048]{2,1,0:T(8,128)(2,1)}), bf16[4,256,2048]{2,1,0:T(8,128)(2,1)}, u32[]{:S(2)}, u32[]{:S(2)}) %all-to-all-start.2) | async-done | bytes 4194336 | tf_op jit(solution)/shard_map/all_to_all | solution.py:51
  305.7 3.4 convert_reduce_fusion
  309.1 0.8 multiply_reduce_fusion
  310.0 0.7 copy-done.3
  310.7 0.4 multiply_convert_fusion.3
  311.2 8.8 %copy.27 = bf16[16,16,2048]{0,1,2:T(8,128)(2,1)} copy(bf16[16,16,2048]{2,1,0:T(8,128)(2,1)S(1)} %bitcast.81) | data formatting | bytes 2097152 | tf_op jit(solution)/shard_map/reshape | solution.py:67
  320.0 7.5 %bitcast_bitcast_fusion = bf16[2048,16,16]{2,1,0:T(8,128)(2,1)} fusion(bf16[16,16,2048]{0,1,2:T(8,128)(2,1)} %copy.27), kind=kLoop, calls=%fused_computation.71 | loop fusion | bytes 2097152
  327.5 11.2 %reshape.109 = bf16[8,2,32768]{2,1,0:T(2,128)(2,1)} reshape(bf16[2048,16,16]{2,1,0:T(8,128)(2,1)} %bitcast_bitcast_fusion) | data formatting | bytes 2097152
  338.7 5.5 %all-to-all-start.3 = ((bf16[8,2,32768]{2,1,0:T(2,128)(2,1)}), bf16[8,2,32768]{2,1,0:T(2,128)(2,1)S(1)}, u32[]{:S(2)}, u32[]{:S(2)}) async-start(bf16[8,2,32768]{2,1,0:T(2,128)(2,1)} %reshape.109), calls=%async_computation.3 | async-start | bytes 2097152 | tf_op jit(solution)/shard_map/all_to_all | solution.py:68
  344.2 8.8 %copy.24 = bf16[16,16,2048]{0,1,2:T(8,128)(2,1)} copy(bf16[16,16,2048]{2,1,0:T(8,128)(2,1)S(1)} %bitcast.80) | data formatting | bytes 2097152 | tf_op jit(solution)/shard_map/reshape | solution.py:67
  353.1 7.5 %bitcast_bitcast_fusion.1 = bf16[2048,16,16]{2,1,0:T(8,128)(2,1)} fusion(bf16[16,16,2048]{0,1,2:T(8,128)(2,1)} %copy.24), kind=kLoop, calls=%fused_computation.72 | loop fusion | bytes 2097152
  360.5 11.2 %reshape.111 = bf16[8,2,32768]{2,1,0:T(2,128)(2,1)} reshape(bf16[2048,16,16]{2,1,0:T(8,128)(2,1)} %bitcast_bitcast_fusion.1) | data formatting | bytes 2097152
  371.8 6.0 %all-to-all-start.1 = ((bf16[8,2,32768]{2,1,0:T(2,128)(2,1)}), bf16[8,2,32768]{2,1,0:T(2,128)(2,1)S(1)}, u32[]{:S(2)}, u32[]{:S(2)}) async-start(bf16[8,2,32768]{2,1,0:T(2,128)(2,1)} %reshape.111), calls=%async_computation.1 | async-start | bytes 2097152 | tf_op jit(solution)/shard_map/all_to_all | solution.py:68
  377.8 3.9 fusion.24
  381.8 4.0 fusion.23
  385.9 0.7 maximum_bitcast_fusion.1
  386.5 7.6 %reshape.110 = bf16[2048,16,16]{2,1,0:T(8,128)(2,1)} reshape(bf16[8,2,32768]{2,1,0:T(2,128)(2,1)S(1)} %all-to-all-done.3) | data formatting | bytes 2097152
  394.1 9.1 %copy.29 = bf16[16,256,8,16]{1,3,2,0:T(8,128)(2,1)} copy(bf16[16,256,8,16]{3,0,1,2:T(8,128)(2,1)} %bitcast.72) | data formatting | bytes 2097152 | tf_op jit(solution)/shard_map/all_to_all | solution.py:68
  403.2 7.6 %reshape.112 = bf16[2048,16,16]{2,1,0:T(8,128)(2,1)} reshape(bf16[8,2,32768]{2,1,0:T(2,128)(2,1)S(1)} %all-to-all-done.1) | data formatting | bytes 2097152
  410.8 9.1 %copy.26 = bf16[16,256,8,16]{1,3,2,0:T(8,128)(2,1)} copy(bf16[16,256,8,16]{3,0,1,2:T(8,128)(2,1)} %bitcast.73) | data formatting | bytes 2097152 | tf_op jit(solution)/shard_map/all_to_all | solution.py:68
  419.9 1.7 maximum_bitcast_fusion
  421.6 2.4 copy.30
  (47 shorter events, 0.6 us)
Async XLA Ops:
  7.2 263.8 %copy-start = (bf16[256,2048]{1,0:T(8,128)(2,1)S(1)}, bf16[256,2048]{1,0:T(8,128)(2,1)}, u32[]{:S(2)}) copy-start(bf16[256,2048]{1,0:T(8,128)(2,1)} %param.16) | copy-start | bytes 3145732
  7.2 4.8 %copy-start.14 = (s32[1,2]{1,0:T(1,128)S(1)}, s32[1,2]{1,0:T(1,128)}, u32[]{:S(2)}) copy-start(s32[1,2]{1,0:T(1,128)} %param.13) | copy-start | bytes 28
  7.2 10.7 %copy-start.11 = (bf16[1,2048]{1,0:T(2,128)(2,1)S(1)}, bf16[1,2048]{1,0:T(2,128)(2,1)}, u32[]{:S(2)}) copy-start(bf16[1,2048]{1,0:T(2,128)(2,1)} %param.15) | copy-start | bytes 12292
  7.2 40.6 %all-gather.6.cloned.1.call-start = ((), (), s32[]{:S(2)}) async-start(), calls=%async_computation.4 | async-start | bytes 5242880 | tf_op jit(solution)/shard_map/all_gather | solution.py:44
  10.5 164.4 %all-gather.10.cloned.1.call-start = ((), (), s32[]{:S(2)}) async-start(), calls=%async_computation.6 | async-start | bytes 9437184 | tf_op jit(solution)/shard_map/all_gather | solution.py:35
  11.2 206.8 %all-gather.8.cloned.1.call-start = ((), (), s32[]{:S(2)}) async-start(), calls=%async_computation.5 | async-start | bytes 5242880 | tf_op jit(solution)/shard_map/all_gather | solution.py:44
  190.7 61.9 %all-to-all-start = ((bf16[4,256,2048]{2,1,0:T(8,128)(2,1)}), bf16[4,256,2048]{2,1,0:T(8,128)(2,1)}, u32[]{:S(2)}, u32[]{:S(2)}) async-start(bf16[4,256,2048]{2,1,0:T(8,128)(2,1)} %multiply_convert_fusion.1), calls=%async_computation | async-start | bytes 8388608 | tf_op jit(solution)/shard_map/all_to_all | solution.py:51
  218.0 3.4 copy-start.7
  235.9 21.7 %copy-start.10 = (s32[1,2,2,16,16]{4,3,2,1,0:T(8,128)S(1)}, s32[1,2,2,16,16]{4,3,2,1,0:T(8,128)}, u32[]{:S(2)}) copy-start(s32[1,2,2,16,16]{4,3,2,1,0:T(8,128)} %param.12) | copy-start | bytes 12292
  235.9 21.9 %copy-start.4 = (bf16[1,2,16,16,2048]{4,3,2,1,0:T(8,128)(2,1)S(1)}, bf16[1,2,16,16,2048]{4,3,2,1,0:T(8,128)(2,1)}, u32[]{:S(2)}) copy-start(bf16[1,2,16,16,2048]{4,3,2,1,0:T(8,128)(2,1)} %param.10) | copy-start | bytes 6291460
  235.9 22.4 %copy-start.12 = (bf16[2048]{0:T(1024)(128)(2,1)S(1)}, bf16[2048]{0:T(1024)(128)(2,1)}, u32[]{:S(2)}) copy-start(bf16[2048]{0:T(1024)(128)(2,1)} %param.17) | copy-start | bytes 12292
  252.6 53.1 %all-to-all-start.2 = ((bf16[4,256,2048]{2,1,0:T(8,128)(2,1)}), bf16[4,256,2048]{2,1,0:T(8,128)(2,1)}, u32[]{:S(2)}, u32[]{:S(2)}) async-start(bf16[4,256,2048]{2,1,0:T(8,128)(2,1)} %multiply_convert_fusion), calls=%async_computation.2 | async-start | bytes 8388608 | tf_op jit(solution)/shard_map/all_to_all | solution.py:51
  266.1 4.9 %copy-start.5 = (f32[512,2048]{1,0:T(8,128)}, f32[512,2048]{1,0:T(8,128)S(1)}, u32[]{:S(2)}) copy-start(f32[512,2048]{1,0:T(8,128)S(1)} %bitcast_add_fusion) | copy-start | bytes 12582916
  266.1 4.9 %copy-start.2 = (bf16[1,1,16,16,2048]{4,3,2,1,0:T(8,128)(2,1)S(1)}, bf16[1,1,16,16,2048]{4,3,2,1,0:T(8,128)(2,1)}, u32[]{:S(2)}) copy-start(bf16[1,1,16,16,2048]{4,3,2,1,0:T(8,128)(2,1)} %get-tuple-element.8) | copy-start | bytes 3145732
  273.1 36.0 %copy-start.1 = (bf16[1,1,16,16,2048]{4,3,2,1,0:T(8,128)(2,1)S(1)}, bf16[1,1,16,16,2048]{4,3,2,1,0:T(8,128)(2,1)}, u32[]{:S(2)}) copy-start(bf16[1,1,16,16,2048]{4,3,2,1,0:T(8,128)(2,1)} %get-tuple-element.9) | copy-start | bytes 3145732
  305.7 3.4 copy-start.6
  309.1 1.6 copy-start.3
  311.1 8.8 %copy-start.9 = (bf16[256,2048]{1,0:T(8,128)(2,1)}, bf16[256,2048]{1,0:T(8,128)(2,1)S(1)}, u32[]{:S(2)}) copy-start(bf16[256,2048]{1,0:T(8,128)(2,1)S(1)} %get-tuple-element.15) | copy-start | bytes 3145732
  311.2 33.1 %copy-start.8 = (bf16[256,2048]{1,0:T(8,128)(2,1)}, bf16[256,2048]{1,0:T(8,128)(2,1)S(1)}, u32[]{:S(2)}) copy-start(bf16[256,2048]{1,0:T(8,128)(2,1)S(1)} %get-tuple-element.14) | copy-start | bytes 3145732
  338.7 33.1 %all-to-all-start.3 = ((bf16[8,2,32768]{2,1,0:T(2,128)(2,1)}), bf16[8,2,32768]{2,1,0:T(2,128)(2,1)S(1)}, u32[]{:S(2)}, u32[]{:S(2)}) async-start(bf16[8,2,32768]{2,1,0:T(2,128)(2,1)} %reshape.109), calls=%async_computation.3 | async-start | bytes 2097152 | tf_op jit(solution)/shard_map/all_to_all | solution.py:68
  360.5 17.2 %copy-start.13 = (bf16[1024]{0:T(1024)(128)(2,1)S(1)}, bf16[1024]{0:T(1024)(128)(2,1)}, u32[]{:S(2)}) copy-start(bf16[1024]{0:T(1024)(128)(2,1)} %param.19) | copy-start | bytes 6148
  371.8 31.4 %all-to-all-start.1 = ((bf16[8,2,32768]{2,1,0:T(2,128)(2,1)}), bf16[8,2,32768]{2,1,0:T(2,128)(2,1)S(1)}, u32[]{:S(2)}, u32[]{:S(2)}) async-start(bf16[8,2,32768]{2,1,0:T(2,128)(2,1)} %reshape.111), calls=%async_computation.1 | async-start | bytes 2097152 | tf_op jit(solution)/shard_map/all_to_all | solution.py:68
Sparse Core Ops, SparseCore 0:
  10.6 37.1 all-gather.5
  49.9 124.9 all-gather.9
  176.5 41.4 all-gather.7
where the time goes:
time: 432 us; the launch traced here: 431 us
  waiting for transfers between devices  227 us (53%)
  local copies, waits for them, and re-layouts  95.7 us (22%)
  matrix products  41.7 us (10%)
  other arithmetic  24.9 us (6%)
  starting transfers between devices  21.6 us (5%)
  between operations  14 us (3%)
  blocking collectives  5.95 us (1%)
    all_gather x1, waiting for transfers between devices, local(): own_whole = lax.all_gather(weight_shard, 'env', axis=0, tiled=True)  124 us
    unnamed x38, local copies, waits for them, and re-layouts  56 us
    all_gather x2, waiting for transfers between devices, local(): all_rows = lax.all_gather(opp_raw, 'league', axis=0, tiled=True)  52.1 us
    all_to_all x2, waiting for transfers between devices, local(): lax.all_to_all(products, 'league', split_axis=0, concat_axis=0, tiled=True)  49.2 us
    dot_general x2, matrix products, local(): jnp.dot(all_normed, own_whole, preferred_element_type=jnp.float32)  23.9 us
    all_to_all x2, local copies, waits for them, and re-layouts, local(): lax.all_to_all(time_block, 'env', split_axis=1, concat_axis=2, tiled=True)  18.2 us
    reshape x2, local copies, waits for them, and re-layouts, local(): joint_row.reshape(env_count, step_count, model_width).transpose(1, 2, 0)  17.7 us
    all_to_all x2, starting transfers between devices, local(): lax.all_to_all(time_block, 'env', split_axis=1, concat_axis=2, tiled=True)  11.5 us
  transfers between devices with their start and end apart: 7, of which 5 were waited for; matrix products, arithmetic and copies ran while one was open for 24% of the time, Pallas kernels for 0%

commit v1 on v0

--- a/solution.py
+++ b/solution.py
@@ -2,6 +2,22 @@
 import jax.numpy as jnp
 from jax import lax
 from jax.sharding import PartitionSpec as P
+
+
+def pairwise_exchange(shard, axis, split, join):
+    ways, here = (lax.axis_size(axis), lax.axis_index(axis))
+    width = shard.shape[split] // ways
+    lengths = list(shard.shape)
+    lengths[split] = width
+    height = lengths[join]
+    lengths[join] = height * ways
+    full = jnp.zeros(lengths, shard.dtype)
+    for mask in range(ways):
+        part = lax.dynamic_slice_in_dim(shard, (here ^ mask) * width, width, axis=split)
+        if mask:
+            part = lax.ppermute(part, axis, [(d, d ^ mask) for d in range(ways)])
+        full = lax.dynamic_update_slice_in_dim(full, part, (here ^ mask) * height, axis=join)
+    return full
 
 
 def rms_norm(inputs, gain):
@@ -65,7 +81,7 @@
         value_est = jnp.dot(value_hidden, value_out, preferred_element_type=jnp.float32)
         value_list.append(value_est.reshape(env_count, step_count))
         time_block = joint_row.reshape(env_count, step_count, model_width).transpose(1, 2, 0)
-        traj_list.append(lax.all_to_all(time_block, "env", split_axis=1, concat_axis=2, tiled=True))
+        traj_list.append(pairwise_exchange(time_block, "env", 1, 2))
     learner_rows = jnp.stack(traj_list)
     values = jnp.stack(value_list)
     return (learner_rows[None], values[None])

time: 432 us -> 584 us (1.35)
  local copies, waits for them, and re-layouts: 95.7 us -> 227 us
  starting transfers between devices: 21.6 us -> 37.5 us
    dynamic_update_slice x0 -> x16, local copies, waits for them, and re-layouts: none -> 179 us  [pairwise_exchange(): lax.dynamic_update_slice_in_dim(full, part, (here ^ mask) * height, axis=...]
    unnamed x38 -> x47, local copies, waits for them, and re-layouts: 56 us -> 12.8 us
    another operation x0 -> x18, local copies, waits for them, and re-layouts: none -> 31.3 us  [the longest x16 30.2 us: local(): learner_rows = jnp.stack(traj_list)]
    ppermute x0 -> x14, starting transfers between devices: none -> 27.5 us  [pairwise_exchange(): part = lax.ppermute(part, axis, [(d, d ^ mask) for d in range(ways)])]
    all_to_all x2 -> x0, local copies, waits for them, and re-layouts: 18.2 us -> none  [local(): lax.all_to_all(time_block, 'env', split_axis=1, concat_axis=2, tiled=True)]
    reshape x2 -> x0, local copies, waits for them, and re-layouts: 17.7 us -> none  [local(): joint_row.reshape(env_count, step_count, model_width).transpose(1, 2, 0)]
    all_to_all x2 -> x0, starting transfers between devices: 11.5 us -> none  [local(): lax.all_to_all(time_block, 'env', split_axis=1, concat_axis=2, tiled=True)]
  transfers between devices with their start and end apart: 7 -> 19, of which waited for: 5 -> 5; matrix products, arithmetic and copies ran while one was open for 24% -> 20% of each run, Pallas kernels for 0% -> 0%
where the time goes in v1:
time: 584 us; the launch traced here: 579 us
  local copies, waits for them, and re-layouts  227 us (39%)
  waiting for transfers between devices  227 us (39%)
  matrix products  41 us (7%)
  starting transfers between devices  37.5 us (6%)
  other arithmetic  26.2 us (4%)
  between operations  14.2 us (2%)
  blocking collectives  5.95 us (1%)
    dynamic_update_slice x16, local copies, waits for them, and re-layouts, pairwise_exchange(): lax.dynamic_update_slice_in_dim(full, part, (here ^ mask) * height, axis=...  179 us
    all_gather x1, waiting for transfers between devices, local(): own_whole = lax.all_gather(weight_shard, 'env', axis=0, tiled=True)  124 us
    all_gather x2, waiting for transfers between devices, local(): all_rows = lax.all_gather(opp_raw, 'league', axis=0, tiled=True)  52.1 us
    all_to_all x2, waiting for transfers between devices, local(): lax.all_to_all(products, 'league', split_axis=0, concat_axis=0, tiled=True)  49.1 us
    another operation x16, local copies, waits for them, and re-layouts, local(): learner_rows = jnp.stack(traj_list)  30.2 us
    ppermute x14, starting transfers between devices, pairwise_exchange(): part = lax.ppermute(part, axis, [(d, d ^ mask) for d in range(ways)])  27.5 us
    dot_general x2, matrix products, local(): jnp.dot(all_normed, own_whole, preferred_element_type=jnp.float32)  23.9 us
    unnamed x47, local copies, waits for them, and re-layouts  12.8 us
  transfers between devices with their start and end apart: 19, of which 5 were waited for; matrix products, arithmetic and copies ran while one was open for 20% of the time, Pallas kernels for 0%

profile of v1, /device:TPU:0, one launch (start us, length us, event | category | flops | bytes accessed | tf_op | source)
XLA Modules:
  0.0 578.6 jit_solution(15126745250628249159)
XLA Ops:
  7.2 3.2 fusion.43
  11.9 6.0 %all-gather.1 = s32[4,1,2]{2,1,0:T(1,128)S(1)} all-gather(s32[1,1,2]{2,1,0:T(1,128)S(1)} %bitcast.135), channel_id=1, replica_groups=mesh['league'=4,'env'=8] {'league'}, dimensions={0}, use_global_device_ids=true | all-gather | bytes 40 | tf_op jit(solution)/shard_map/all_gather | solution.py:53
  18.0 29.8 %all-gather.8.cloned.1.call-done = bf16[1024,2048]{1,0:T(8,128)(2,1)} async-done(((bf16[256,2048]{1,0:T(8,128)(2,1)}), bf16[1024,2048]{1,0:T(8,128)(2,1)}) %all-gather.8.cloned.1.call-update) | async-done | bytes 4194320 | tf_op jit(solution)/shard_map/all_gather | solution.py:60
  47.8 3.1 fusion.3
  50.9 124.0 %all-gather.10.cloned.1.call-done = bf16[1,2048,2048]{2,1,0:T(8,128)(2,1)} async-done(((bf16[1,256,2048]{2,1,0:T(8,128)(2,1)}), bf16[1,2048,2048]{2,1,0:T(8,128)(2,1)}) %all-gather.10.cloned.1.call-update) | async-done | bytes 8388624 | tf_op jit(solution)/shard_map/all_gather | solution.py:51
  174.9 12.6 %fusion.6 = f32[1024,2048]{1,0:T(8,128)S(1)} fusion(bf16[1,2048,2048]{2,1,0:T(8,128)(2,1)} %all-gather.10.cloned.1.call-done, bf16[1024,2048]{1,0:T(8,128)(2,1)} %all-gather.8.cloned.1.call-done, f32[1024]{0:T(1024)S(1)} %add_rsqrt_fusion.1, f32[2048]{0:T(1024)S(1)} %bitcast.129), kind=kOutput, calls=%fused_computation.10 | convolution fusion | flops 8598323200 | bytes 20983808 | tf_op jit(solution)/shard_map/dot_general | solution.py:62
  187.5 3.2 multiply_convert_fusion
  190.7 4.9 all-to-all-start.1
  195.6 22.3 %all-gather.6.cloned.1.call-done = bf16[1024,2048]{1,0:T(8,128)(2,1)} async-done(((bf16[256,2048]{1,0:T(8,128)(2,1)}), bf16[1024,2048]{1,0:T(8,128)(2,1)}) %all-gather.6.cloned.1.call-update) | async-done | bytes 4194320 | tf_op jit(solution)/shard_map/all_gather | solution.py:60
  218.0 3.2 fusion
  221.4 11.3 %fusion.8 = f32[1024,2048]{1,0:T(8,128)S(1)} fusion(bf16[1,2048,2048]{2,1,0:T(8,128)(2,1)} %all-gather.10.cloned.1.call-done, bf16[1024,2048]{1,0:T(8,128)(2,1)S(1)} %copy-done.8, f32[2048]{0:T(1024)S(1)} %bitcast.130, f32[1024]{0:T(1024)S(1)} %add_rsqrt_fusion.2), kind=kOutput, calls=%fused_computation.12 | convolution fusion | flops 8598323200 | bytes 20983808 | tf_op jit(solution)/shard_map/dot_general | solution.py:62
  232.7 3.2 multiply_convert_fusion.1
  236.0 16.6 %all-to-all-done.1 = bf16[4,256,2048]{2,1,0:T(8,128)(2,1)} async-done(((bf16[4,256,2048]{2,1,0:T(8,128)(2,1)}), bf16[4,256,2048]{2,1,0:T(8,128)(2,1)}, u32[]{:S(2)}, u32[]{:S(2)}) %all-to-all-start.1) | async-done | bytes 4194336 | tf_op jit(solution)/shard_map/all_to_all | solution.py:67
  252.6 5.0 all-to-all-start
  259.2 7.0 %bitcast_add_fusion = f32[512,2048]{1,0:T(8,128)S(1)} fusion(bf16[1,2,16,16,2048]{4,3,2,1,0:T(8,128)(2,1)S(1)} %copy-done.4, bf16[512,2048]{1,0:T(8,128)(2,1)S(1)} %fusion.16, bf16[1,2048,2048]{2,1,0:T(8,128)(2,1)} %all-gather.10.cloned.1.call-done), kind=kOutput, calls=%fused_computation.20 | convolution fusion | flops 4297064448 | bytes 16777216 | tf_op jit(solution)/shard_map/dot_general | solution.py:52
  266.2 4.8 convert_reduce_fusion
  273.2 32.5 %all-to-all-done = bf16[4,256,2048]{2,1,0:T(8,128)(2,1)} async-done(((bf16[4,256,2048]{2,1,0:T(8,128)(2,1)}), bf16[4,256,2048]{2,1,0:T(8,128)(2,1)}, u32[]{:S(2)}, u32[]{:S(2)}) %all-to-all-start) | async-done | bytes 4194336 | tf_op jit(solution)/shard_map/all_to_all | solution.py:67
  305.7 3.4 convert_reduce_fusion.1
  315.2 2.5 collective-permute-start.3
  323.4 3.3 collective-permute-start.5
  328.7 3.6 collective-permute-start.8
  332.3 3.6 fusion.23
  345.0 3.7 collective-permute-start.10
  349.1 4.3 collective-permute-start.12
  354.0 3.6 fusion.24
  360.0 9.2 %dynamic_update_slice.64 = bf16[1,16,256,128]{3,2,1,0:T(8,128)(2,1)} dynamic-update-slice(bf16[1,16,256,128]{3,2,1,0:T(8,128)(2,1)} %stack.42.clone.1, bf16[1,16,256,16]{3,2,1,0:T(8,128)(2,1)S(1)} %bitcast.121, s32[]{:T(128)} %constant.55.clone.1, s32[]{:T(128)} %constant.55.clone.1, s32[]{:T(128)} %constant.55.clone.1, s32[]{:T(128)S(6)} %select_n.65) | dynamic-update-slice | bytes 262148 | tf_op jit(solution)/shard_map/dynamic_update_slice | solution.py:19
  369.5 3.7 dynamic_update_slice.72
  373.9 2.2 copy.32
  376.1 2.3 copy.34
  378.5 2.3 copy.36
  382.9 2.2 copy.40
  390.2 2.3 copy.49
  393.8 2.3 copy.53
  402.7 12.0 %dynamic_update_slice.65 = bf16[1,16,256,128]{3,2,1,0:T(8,128)(2,1)} dynamic-update-slice(bf16[1,16,256,128]{3,2,1,0:T(8,128)(2,1)} %dynamic_update_slice.64, bf16[1,16,256,16]{3,2,1,0:T(8,128)(2,1)} %copy.32, s32[]{:T(128)} %constant.55.clone.1, s32[]{:T(128)} %constant.55.clone.1, s32[]{:T(128)} %constant.55.clone.1, s32[]{:T(128)S(6)} %select_n.67) | dynamic-update-slice | bytes 262148 | tf_op jit(solution)/shard_map/dynamic_update_slice | solution.py:19
  414.7 12.0 %dynamic_update_slice.73 = bf16[1,16,256,128]{3,2,1,0:T(8,128)(2,1)} dynamic-update-slice(bf16[1,16,256,128]{3,2,1,0:T(8,128)(2,1)} %copy-done.9, bf16[1,16,256,16]{3,2,1,0:T(8,128)(2,1)} %copy.47, s32[]{:T(128)} %constant.55.clone.1, s32[]{:T(128)} %constant.55.clone.1, s32[]{:T(128)} %constant.55.clone.1, s32[]{:T(128)S(6)} %select_n.67) | dynamic-update-slice | bytes 262148 | tf_op jit(solution)/shard_map/dynamic_update_slice | solution.py:19
  426.7 12.0 %dynamic_update_slice.66 = bf16[1,16,256,128]{3,2,1,0:T(8,128)(2,1)} dynamic-update-slice(bf16[1,16,256,128]{3,2,1,0:T(8,128)(2,1)} %dynamic_update_slice.65, bf16[1,16,256,16]{3,2,1,0:T(8,128)(2,1)} %copy.34, s32[]{:T(128)} %constant.55.clone.1, s32[]{:T(128)} %constant.55.clone.1, s32[]{:T(128)} %constant.55.clone.1, s32[]{:T(128)S(6)} %select_n.69) | dynamic-update-slice | bytes 262148 | tf_op jit(solution)/shard_map/dynamic_update_slice | solution.py:19
  438.7 12.0 %dynamic_update_slice.74 = bf16[1,16,256,128]{3,2,1,0:T(8,128)(2,1)} dynamic-update-slice(bf16[1,16,256,128]{3,2,1,0:T(8,128)(2,1)} %dynamic_update_slice.73, bf16[1,16,256,16]{3,2,1,0:T(8,128)(2,1)} %copy.49, s32[]{:T(128)} %constant.55.clone.1, s32[]{:T(128)} %constant.55.clone.1, s32[]{:T(128)} %constant.55.clone.1, s32[]{:T(128)S(6)} %select_n.69) | dynamic-update-slice | bytes 262148 | tf_op jit(solution)/shard_map/dynamic_update_slice | solution.py:19
  450.7 12.0 %dynamic_update_slice.67 = bf16[1,16,256,128]{3,2,1,0:T(8,128)(2,1)} dynamic-update-slice(bf16[1,16,256,128]{3,2,1,0:T(8,128)(2,1)} %dynamic_update_slice.66, bf16[1,16,256,16]{3,2,1,0:T(8,128)(2,1)} %copy.36, s32[]{:T(128)} %constant.55.clone.1, s32[]{:T(128)} %constant.55.clone.1, s32[]{:T(128)} %constant.55.clone.1, s32[]{:T(128)S(6)} %select_n.71) | dynamic-update-slice | bytes 262148 | tf_op jit(solution)/shard_map/dynamic_update_slice | solution.py:19
  462.7 12.0 %dynamic_update_slice.75 = bf16[1,16,256,128]{3,2,1,0:T(8,128)(2,1)} dynamic-update-slice(bf16[1,16,256,128]{3,2,1,0:T(8,128)(2,1)} %dynamic_update_slice.74, bf16[1,16,256,16]{3,2,1,0:T(8,128)(2,1)} %copy.51, s32[]{:T(128)} %constant.55.clone.1, s32[]{:T(128)} %constant.55.clone.1, s32[]{:T(128)} %constant.55.clone.1, s32[]{:T(128)S(6)} %select_n.71) | dynamic-update-slice | bytes 262148 | tf_op jit(solution)/shard_map/dynamic_update_slice | solution.py:19
  474.7 12.0 %dynamic_update_slice.68 = bf16[1,16,256,128]{3,2,1,0:T(8,128)(2,1)} dynamic-update-slice(bf16[1,16,256,128]{3,2,1,0:T(8,128)(2,1)} %dynamic_update_slice.67, bf16[1,16,256,16]{3,2,1,0:T(8,128)(2,1)} %copy.38, s32[]{:T(128)} %constant.55.clone.1, s32[]{:T(128)} %constant.55.clone.1, s32[]{:T(128)} %constant.55.clone.1, s32[]{:T(128)S(6)} %select_n.73) | dynamic-update-slice | bytes 262148 | tf_op jit(solution)/shard_map/dynamic_update_slice | solution.py:19
  486.7 12.0 %dynamic_update_slice.76 = bf16[1,16,256,128]{3,2,1,0:T(8,128)(2,1)} dynamic-update-slice(bf16[1,16,256,128]{3,2,1,0:T(8,128)(2,1)} %dynamic_update_slice.75, bf16[1,16,256,16]{3,2,1,0:T(8,128)(2,1)} %copy.53, s32[]{:T(128)} %constant.55.clone.1, s32[]{:T(128)} %constant.55.clone.1, s32[]{:T(128)} %constant.55.clone.1, s32[]{:T(128)S(6)} %select_n.73) | dynamic-update-slice | bytes 262148 | tf_op jit(solution)/shard_map/dynamic_update_slice | solution.py:19
  498.7 12.0 %dynamic_update_slice.69 = bf16[1,16,256,128]{3,2,1,0:T(8,128)(2,1)} dynamic-update-slice(bf16[1,16,256,128]{3,2,1,0:T(8,128)(2,1)} %dynamic_update_slice.68, bf16[1,16,256,16]{3,2,1,0:T(8,128)(2,1)} %copy.40, s32[]{:T(128)} %constant.55.clone.1, s32[]{:T(128)} %constant.55.clone.1, s32[]{:T(128)} %constant.55.clone.1, s32[]{:T(128)S(6)} %select_n.75) | dynamic-update-slice | bytes 262148 | tf_op jit(solution)/shard_map/dynamic_update_slice | solution.py:19
  510.7 12.0 %dynamic_update_slice.77 = bf16[1,16,256,128]{3,2,1,0:T(8,128)(2,1)} dynamic-update-slice(bf16[1,16,256,128]{3,2,1,0:T(8,128)(2,1)} %dynamic_update_slice.76, bf16[1,16,256,16]{3,2,1,0:T(8,128)(2,1)} %copy.55, s32[]{:T(128)} %constant.55.clone.1, s32[]{:T(128)} %constant.55.clone.1, s32[]{:T(128)} %constant.55.clone.1, s32[]{:T(128)S(6)} %select_n.75) | dynamic-update-slice | bytes 262148 | tf_op jit(solution)/shard_map/dynamic_update_slice | solution.py:19
  522.7 11.4 %dynamic_update_slice.70 = bf16[1,16,256,128]{3,2,1,0:T(8,128)(2,1)} dynamic-update-slice(bf16[1,16,256,128]{3,2,1,0:T(8,128)(2,1)} %dynamic_update_slice.69, bf16[1,16,256,16]{3,2,1,0:T(8,128)(2,1)S(1)} %copy.42, s32[]{:T(128)} %constant.55.clone.1, s32[]{:T(128)} %constant.55.clone.1, s32[]{:T(128)} %constant.55.clone.1, s32[]{:T(128)S(6)} %select_n.77) | dynamic-update-slice | bytes 262148 | tf_op jit(solution)/shard_map/dynamic_update_slice | solution.py:19
  534.1 12.1 %dynamic_update_slice.78 = bf16[1,16,256,128]{3,2,1,0:T(8,128)(2,1)} dynamic-update-slice(bf16[1,16,256,128]{3,2,1,0:T(8,128)(2,1)} %dynamic_update_slice.77, bf16[1,16,256,16]{3,2,1,0:T(8,128)(2,1)} %copy.57, s32[]{:T(128)} %constant.55.clone.1, s32[]{:T(128)} %constant.55.clone.1, s32[]{:T(128)} %constant.55.clone.1, s32[]{:T(128)S(6)} %select_n.77) | dynamic-update-slice | bytes 262148 | tf_op jit(solution)/shard_map/dynamic_update_slice | solution.py:19
  546.2 11.4 %dynamic_update_slice.71 = bf16[1,16,256,128]{3,2,1,0:T(8,128)(2,1)} dynamic-update-slice(bf16[1,16,256,128]{3,2,1,0:T(8,128)(2,1)} %dynamic_update_slice.70, bf16[1,16,256,16]{3,2,1,0:T(8,128)(2,1)S(1)} %copy.44, s32[]{:T(128)} %constant.55.clone.1, s32[]{:T(128)} %constant.55.clone.1, s32[]{:T(128)} %constant.55.clone.1, s32[]{:T(128)S(6)} %select_n.79) | dynamic-update-slice | bytes 262148 | tf_op jit(solution)/shard_map/dynamic_update_slice | solution.py:19
  557.6 11.4 %dynamic_update_slice.79 = bf16[1,16,256,128]{3,2,1,0:T(8,128)(2,1)} dynamic-update-slice(bf16[1,16,256,128]{3,2,1,0:T(8,128)(2,1)} %dynamic_update_slice.78, bf16[1,16,256,16]{3,2,1,0:T(8,128)(2,1)S(1)} %copy-done.7, s32[]{:T(128)} %constant.55.clone.1, s32[]{:T(128)} %constant.55.clone.1, s32[]{:T(128)} %constant.55.clone.1, s32[]{:T(128)S(6)} %select_n.79) | dynamic-update-slice | bytes 262148 | tf_op jit(solution)/shard_map/dynamic_update_slice | solution.py:19
  569.0 3.1 maximum_bitcast_fusion
  (110 shorter events, 47.7 us)
Async XLA Ops:
  7.2 263.9 %copy-start = (bf16[256,2048]{1,0:T(8,128)(2,1)S(1)}, bf16[256,2048]{1,0:T(8,128)(2,1)}, u32[]{:S(2)}) copy-start(bf16[256,2048]{1,0:T(8,128)(2,1)} %param.16) | copy-start | bytes 3145732
  7.2 4.8 copy-start.14
  7.2 10.7 %copy-start.11 = (bf16[1,2048]{1,0:T(2,128)(2,1)S(1)}, bf16[1,2048]{1,0:T(2,128)(2,1)}, u32[]{:S(2)}) copy-start(bf16[1,2048]{1,0:T(2,128)(2,1)} %param.15) | copy-start | bytes 12292
  7.2 40.6 %all-gather.8.cloned.1.call-start = ((), (), s32[]{:S(2)}) async-start(), calls=%async_computation.3 | async-start | bytes 5242880 | tf_op jit(solution)/shard_map/all_gather | solution.py:60
  10.5 164.4 %all-gather.10.cloned.1.call-start = ((), (), s32[]{:S(2)}) async-start(), calls=%async_computation.4 | async-start | bytes 9437184 | tf_op jit(solution)/shard_map/all_gather | solution.py:51
  11.2 206.7 %all-gather.6.cloned.1.call-start = ((), (), s32[]{:S(2)}) async-start(), calls=%async_computation.2 | async-start | bytes 5242880 | tf_op jit(solution)/shard_map/all_gather | solution.py:60
  190.7 61.9 %all-to-all-start.1 = ((bf16[4,256,2048]{2,1,0:T(8,128)(2,1)}), bf16[4,256,2048]{2,1,0:T(8,128)(2,1)}, u32[]{:S(2)}, u32[]{:S(2)}) async-start(bf16[4,256,2048]{2,1,0:T(8,128)(2,1)} %multiply_convert_fusion), calls=%async_computation.1 | async-start | bytes 8388608 | tf_op jit(solution)/shard_map/all_to_all | solution.py:67
  217.9 3.4 copy-start.8
  236.0 21.7 %copy-start.4 = (bf16[1,2,16,16,2048]{4,3,2,1,0:T(8,128)(2,1)S(1)}, bf16[1,2,16,16,2048]{4,3,2,1,0:T(8,128)(2,1)}, u32[]{:S(2)}) copy-start(bf16[1,2,16,16,2048]{4,3,2,1,0:T(8,128)(2,1)} %param.10) | copy-start | bytes 6291460
  236.0 22.2 %copy-start.10 = (s32[1,2,2,16,16]{4,3,2,1,0:T(8,128)S(1)}, s32[1,2,2,16,16]{4,3,2,1,0:T(8,128)}, u32[]{:S(2)}) copy-start(s32[1,2,2,16,16]{4,3,2,1,0:T(8,128)} %param.12) | copy-start | bytes 12292
  236.0 22.6 %copy-start.12 = (bf16[2048]{0:T(1024)(128)(2,1)S(1)}, bf16[2048]{0:T(1024)(128)(2,1)}, u32[]{:S(2)}) copy-start(bf16[2048]{0:T(1024)(128)(2,1)} %param.17) | copy-start | bytes 12292
  236.0 22.6 %copy-start.13 = (bf16[1024]{0:T(1024)(128)(2,1)S(1)}, bf16[1024]{0:T(1024)(128)(2,1)}, u32[]{:S(2)}) copy-start(bf16[1024]{0:T(1024)(128)(2,1)} %param.19) | copy-start | bytes 6148
  252.6 53.1 %all-to-all-start = ((bf16[4,256,2048]{2,1,0:T(8,128)(2,1)}), bf16[4,256,2048]{2,1,0:T(8,128)(2,1)}, u32[]{:S(2)}, u32[]{:S(2)}) async-start(bf16[4,256,2048]{2,1,0:T(8,128)(2,1)} %multiply_convert_fusion.1), calls=%async_computation | async-start | bytes 8388608 | tf_op jit(solution)/shard_map/all_to_all | solution.py:67
  266.2 4.9 copy-start.5
  266.2 4.9 copy-start.2
  273.2 35.9 %copy-start.1 = (bf16[1,1,16,16,2048]{4,3,2,1,0:T(8,128)(2,1)S(1)}, bf16[1,1,16,16,2048]{4,3,2,1,0:T(8,128)(2,1)}, u32[]{:S(2)}) copy-start(bf16[1,1,16,16,2048]{4,3,2,1,0:T(8,128)(2,1)} %get-tuple-element.2) | copy-start | bytes 3145732
  305.7 3.4 copy-start.6
  309.1 1.6 copy-start.3
  311.4 12.1 %collective-permute-start = (bf16[16,256,16]{1,2,0:T(8,128)(2,1)S(1)}, bf16[16,256,16]{1,2,0:T(8,128)(2,1)}, u32[]{:S(2)}, u32[]{:S(2)}) collective-permute-start(bf16[16,256,16]{1,2,0:T(8,128)(2,1)S(1)} %bitcast.128), channel_id=1, source_target_pairs={{0,1},{1,0},{2,3},{3,2},{4,5},{5,4},{6,7},{7,6},{8,9},{9,8},{10,11... | collective-permute-start | bytes 393224 | tf_op jit(solution)/shard_map/ppermute | solution.py:18
  312.9 13.8 %collective-permute-start.1 = (bf16[16,256,16]{1,2,0:T(8,128)(2,1)S(1)}, bf16[16,256,16]{1,2,0:T(8,128)(2,1)}, u32[]{:S(2)}, u32[]{:S(2)}) collective-permute-start(bf16[16,256,16]{1,2,0:T(8,128)(2,1)S(1)} %bitcast.127), channel_id=1, source_target_pairs={{0,2},{1,3},{2,0},{3,1},{4,6},{5,7},{6,4},{7,5},{8,10},{9,11},{10,... | collective-permute-start | bytes 393224 | tf_op jit(solution)/shard_map/ppermute | solution.py:18
  314.5 12.7 %collective-permute-start.2 = (bf16[16,256,16]{1,2,0:T(8,128)(2,1)S(1)}, bf16[16,256,16]{1,2,0:T(8,128)(2,1)}, u32[]{:S(2)}, u32[]{:S(2)}) collective-permute-start(bf16[16,256,16]{1,2,0:T(8,128)(2,1)S(1)} %bitcast.126), channel_id=1, source_target_pairs={{0,3},{1,2},{2,1},{3,0},{4,7},{5,6},{6,5},{7,4},{8,11},{9,10},{10,... | collective-permute-start | bytes 393224 | tf_op jit(solution)/shard_map/ppermute | solution.py:18
  315.2 13.5 %collective-permute-start.3 = (bf16[16,256,16]{1,2,0:T(8,128)(2,1)S(1)}, bf16[16,256,16]{1,2,0:T(8,128)(2,1)}, u32[]{:S(2)}, u32[]{:S(2)}) collective-permute-start(bf16[16,256,16]{1,2,0:T(8,128)(2,1)S(1)} %bitcast.125), channel_id=1, source_target_pairs={{0,4},{1,5},{2,6},{3,7},{4,0},{5,1},{6,2},{7,3},{8,12},{9,13},{10,... | collective-permute-start | bytes 393224 | tf_op jit(solution)/shard_map/ppermute | solution.py:18
  318.3 24.7 %collective-permute-start.4 = (bf16[16,256,16]{1,2,0:T(8,128)(2,1)}, bf16[16,256,16]{1,2,0:T(8,128)(2,1)}, u32[]{:S(2)}, u32[]{:S(2)}) collective-permute-start(bf16[16,256,16]{1,2,0:T(8,128)(2,1)} %bitcast.109), channel_id=1, source_target_pairs={{0,5},{1,4},{2,7},{3,6},{4,1},{5,0},{6,3},{7,2},{8,13},{9,12},{10,... | collective-permute-start | bytes 393224 | tf_op jit(solution)/shard_map/ppermute | solution.py:18
  323.4 21.6 %collective-permute-start.5 = (bf16[16,256,16]{1,2,0:T(8,128)(2,1)}, bf16[16,256,16]{1,2,0:T(8,128)(2,1)}, u32[]{:S(2)}, u32[]{:S(2)}) collective-permute-start(bf16[16,256,16]{1,2,0:T(8,128)(2,1)} %bitcast.108), channel_id=1, source_target_pairs={{0,6},{1,7},{2,4},{3,5},{4,2},{5,3},{6,0},{7,1},{8,14},{9,15},{10,... | collective-permute-start | bytes 393224 | tf_op jit(solution)/shard_map/ppermute | solution.py:18
  326.7 21.9 %collective-permute-start.6 = (bf16[16,256,16]{1,2,0:T(8,128)(2,1)}, bf16[16,256,16]{1,2,0:T(8,128)(2,1)}, u32[]{:S(2)}, u32[]{:S(2)}) collective-permute-start(bf16[16,256,16]{1,2,0:T(8,128)(2,1)} %bitcast.107), channel_id=1, source_target_pairs={{0,7},{1,6},{2,5},{3,4},{4,3},{5,2},{6,1},{7,0},{8,15},{9,14},{10,... | collective-permute-start | bytes 393224 | tf_op jit(solution)/shard_map/ppermute | solution.py:18
  327.2 21.9 %collective-permute-start.7 = (bf16[16,256,16]{1,2,0:T(8,128)(2,1)}, bf16[16,256,16]{1,2,0:T(8,128)(2,1)}, u32[]{:S(2)}, u32[]{:S(2)}) collective-permute-start(bf16[16,256,16]{1,2,0:T(8,128)(2,1)} %bitcast.106), channel_id=1, source_target_pairs={{0,1},{1,0},{2,3},{3,2},{4,5},{5,4},{6,7},{7,6},{8,9},{9,8},{10,11... | collective-permute-start | bytes 393224 | tf_op jit(solution)/shard_map/ppermute | solution.py:18
  328.7 24.7 %collective-permute-start.8 = (bf16[16,256,16]{1,2,0:T(8,128)(2,1)}, bf16[16,256,16]{1,2,0:T(8,128)(2,1)}, u32[]{:S(2)}, u32[]{:S(2)}) collective-permute-start(bf16[16,256,16]{1,2,0:T(8,128)(2,1)} %bitcast.105), channel_id=1, source_target_pairs={{0,2},{1,3},{2,0},{3,1},{4,6},{5,7},{6,4},{7,5},{8,10},{9,11},{10,... | collective-permute-start | bytes 393224 | tf_op jit(solution)/shard_map/ppermute | solution.py:18
  343.1 49.4 %collective-permute-start.9 = (bf16[16,256,16]{1,2,0:T(8,128)(2,1)}, bf16[16,256,16]{1,2,0:T(8,128)(2,1)S(1)}, u32[]{:S(2)}, u32[]{:S(2)}) collective-permute-start(bf16[16,256,16]{1,2,0:T(8,128)(2,1)} %bitcast.104), channel_id=1, source_target_pairs={{0,3},{1,2},{2,1},{3,0},{4,7},{5,6},{6,5},{7,4},{8,11},{9,10},{10,... | collective-permute-start | bytes 393224 | tf_op jit(solution)/shard_map/ppermute | solution.py:18
  345.0 48.8 %collective-permute-start.10 = (bf16[16,256,16]{1,2,0:T(8,128)(2,1)}, bf16[16,256,16]{1,2,0:T(8,128)(2,1)}, u32[]{:S(2)}, u32[]{:S(2)}) collective-permute-start(bf16[16,256,16]{1,2,0:T(8,128)(2,1)} %bitcast.103), channel_id=1, source_target_pairs={{0,4},{1,5},{2,6},{3,7},{4,0},{5,1},{6,2},{7,3},{8,12},{9,13},{10,... | collective-permute-start | bytes 393224 | tf_op jit(solution)/shard_map/ppermute | solution.py:18
  348.7 47.4 %collective-permute-start.11 = (bf16[16,256,16]{1,2,0:T(8,128)(2,1)}, bf16[16,256,16]{1,2,0:T(8,128)(2,1)}, u32[]{:S(2)}, u32[]{:S(2)}) collective-permute-start(bf16[16,256,16]{1,2,0:T(8,128)(2,1)} %bitcast.102), channel_id=1, source_target_pairs={{0,5},{1,4},{2,7},{3,6},{4,1},{5,0},{6,3},{7,2},{8,13},{9,12},{10,... | collective-permute-start | bytes 393224 | tf_op jit(solution)/shard_map/ppermute | solution.py:18
  349.1 49.2 %collective-permute-start.12 = (bf16[16,256,16]{1,2,0:T(8,128)(2,1)}, bf16[16,256,16]{1,2,0:T(8,128)(2,1)}, u32[]{:S(2)}, u32[]{:S(2)}) collective-permute-start(bf16[16,256,16]{1,2,0:T(8,128)(2,1)} %bitcast.101), channel_id=1, source_target_pairs={{0,6},{1,7},{2,4},{3,5},{4,2},{5,3},{6,0},{7,1},{8,14},{9,15},{10,... | collective-permute-start | bytes 393224 | tf_op jit(solution)/shard_map/ppermute | solution.py:18
  353.4 47.1 %collective-permute-start.13 = (bf16[16,256,16]{1,2,0:T(8,128)(2,1)}, bf16[16,256,16]{1,2,0:T(8,128)(2,1)}, u32[]{:S(2)}, u32[]{:S(2)}) collective-permute-start(bf16[16,256,16]{1,2,0:T(8,128)(2,1)} %bitcast.100), channel_id=1, source_target_pairs={{0,7},{1,6},{2,5},{3,4},{4,3},{5,2},{6,1},{7,0},{8,15},{9,14},{10,... | collective-permute-start | bytes 393224 | tf_op jit(solution)/shard_map/ppermute | solution.py:18
  373.2 12.0 %copy-start.9 = (bf16[1,16,256,128]{3,2,1,0:T(8,128)(2,1)}, bf16[1,16,256,128]{3,2,1,0:T(8,128)(2,1)S(1)}, u32[]{:S(2)}) copy-start(bf16[1,16,256,128]{3,2,1,0:T(8,128)(2,1)S(1)} %dynamic_update_slice.72) | copy-start | bytes 3145732
  534.1 23.5 %copy-start.7 = (bf16[1,16,256,16]{3,2,1,0:T(8,128)(2,1)S(1)}, bf16[1,16,256,16]{3,2,1,0:T(8,128)(2,1)}, u32[]{:S(2)}) copy-start(bf16[1,16,256,16]{3,2,1,0:T(8,128)(2,1)} %copy.59) | copy-start | bytes 393220
Sparse Core Ops, SparseCore 0:
  10.6 37.1 all-gather.7
  49.9 124.9 all-gather.9
  176.4 41.4 all-gather.5
